TPU v7x, 32 devices: a whole 2x2x4 slice. The times are simulated.
32 devices in a mesh: dp: 4 (over z), row: 4 (over y, core), col: 2 (over x).
Axes of the slice: x: 2, y: 2, z: 4, core: 2. Of those that a mesh axis runs over, the one named last changes fastest.
Arguments:
- block_input: bfloat16 [8, 1792, 1024], P('dp', None, ('row', 'col')), may hold values from -45 to 45
- segment_ids: int32 [8, 1792], P('dp'), may hold values from 0 to 3, never falling along the last dimension, each value on 1 to 896 neighbouring positions
- out_grad: bfloat16 [8, 1792, 1024], P('dp', None, ('row', 'col')), may hold values from -6 to 6
- in_weight: bfloat16 [3, 1024, 1024], P(None, 'col', 'row'), may hold values from -0.1875 to 0.1875
- out_weight: bfloat16 [1024, 1024], P('row', 'col'), may hold values from -0.375 to 0.375
- gate_weight: bfloat16 [1024, 4608], P('col', 'row'), may hold values from -0.1875 to 0.1875
- up_weight: bfloat16 [1024, 4608], P('col', 'row'), may hold values from -0.1875 to 0.1875
- down_weight: bfloat16 [4608, 1024], P('row', 'col'), may hold values from -0.1875 to 0.1875
- conv_weight: bfloat16 [3, 1024], P(None, ('row', 'col')), may hold values from -3.5 to 3.5
- mixer_norm_gain: float32 [1024], replicated, may hold values from 0.5 to 1.5
- feedforward_norm_gain: float32 [1024], replicated, may hold values from 0.5 to 1.5
Outputs:
- block_output: bfloat16 [8, 1792, 1024], P('dp', None, ('row', 'col'))
- block_input_gradient: float32 [8, 1792, 1024], P('dp', None, ('row', 'col'))
- grad_in_weight: float32 [3, 1024, 1024], P(None, 'col', 'row')
- grad_out_weight: float32 [1024, 1024], P('row', 'col')
- grad_gate_weight: float32 [1024, 4608], P('col', 'row')
- grad_up_weight: float32 [1024, 4608], P('col', 'row')
- grad_down_weight: float32 [4608, 1024], P('row', 'col')
- grad_conv_weight: float32 [3, 1024], P(None, ('row', 'col'))
- mixer_gain_gradient: float32 [1024], P(('row', 'col'))
- feedforward_gain_gradient: float32 [1024], P(('row', 'col'))
Inputs may be any that keep to these rules, and one draw needn't show every extreme that they name: `segment_ids`: along each sequence the segment numbers never fall; a segment covers at most half of 1792 positions.
All inputs are finite; a program needn't handle non-finite values.
Results may differ from a plain program's by a relative error of at most 0.013.
Values may be sent and summed in bfloat16 or wider, within the bound.
No kernel may reach another device: no remote copies, remote signals or barrier semaphores. Data moves between devices by JAX's collectives and lax.ppermute only.
A program may use at most 256 MiB of HBM per device.

v0:
```python
import jax
import jax.numpy as jnp
from jax import lax
from jax.sharding import PartitionSpec as P

D = 1024
EPS = 1e-05


def lagged(values, shift_by):
    padding = jnp.zeros_like(values[..., :shift_by, :])
    return jnp.concatenate([padding, values[..., :-shift_by, :]], axis=-2)


def leading(values, shift_by):
    padding = jnp.zeros_like(values[..., :shift_by, :])
    return jnp.concatenate([values[..., shift_by:, :], padding], axis=-2)


def same_masks(segments):
    mask_list = []
    for shift_by in (1, 2):
        filler = jnp.full(segments[..., :shift_by].shape, -1, jnp.int32)
        earlier = jnp.concatenate([filler, segments[..., :-shift_by]], axis=-1)
        mask_list.append(jnp.where(earlier == segments, 1.0, 0.0).astype(jnp.float32)[..., None])
    return mask_list


def conv_forward(mixed_in, mask_list, kernel):
    return (
        kernel[0] * mixed_in
        + kernel[1] * mask_list[0] * lagged(mixed_in, 1)
        + kernel[2] * mask_list[1] * lagged(mixed_in, 2)
    )


def conv_backward(d_conved, mixed_in, mask_list, kernel):
    first_term = mask_list[0] * d_conved
    second = mask_list[1] * d_conved
    d_mixed = (
        kernel[0] * d_conved + kernel[1] * leading(first_term, 1) + kernel[2] * leading(second, 2)
    )
    all_axes = tuple(range(d_conved.ndim - 1))
    d_kernel = jnp.stack(
        [
            jnp.sum(d_conved * mixed_in, axis=all_axes),
            jnp.sum(first_term * lagged(mixed_in, 1), axis=all_axes),
            jnp.sum(second * lagged(mixed_in, 2), axis=all_axes),
        ]
    )
    return (d_mixed, d_kernel)


def full_width(part_half):
    return lax.all_gather(part_half, ("row", "col"), axis=1, tiled=True)


def own_share(partial_sum):
    return lax.psum_scatter(partial_sum, ("row", "col"), scatter_dimension=1, tiled=True)


def summed_all(partial_sum):
    return lax.psum(partial_sum, ("row", "col"))


def token_stat(values):
    return lax.psum(jnp.sum(values, axis=1), ("row", "col"))


def full_scale(values):
    return lax.rsqrt(jnp.mean(values * values, axis=1, keepdims=True) + EPS)


def norm_reverse_result(d_normed, x_hat, scale_row, gain_row):
    d_hat = d_normed * gain_row
    mean_term = token_stat(d_hat * x_hat)[:, None] / D
    return scale_row * (d_hat - x_hat * mean_term)


def body(
    block_input,
    segment_ids,
    out_grad,
    in_weight,
    out_weight,
    gate_weight,
    up_weight,
    down_weight,
    conv_weight,
    mixer_norm_gain,
    feedforward_norm_gain,
):
    seq_count, seq_length, own_width = block_input.shape
    tok_rows = seq_count * seq_length
    own_start = (lax.axis_index("row") * lax.axis_size("col") + lax.axis_index("col")) * own_width
    kernel = conv_weight.astype(jnp.float32)
    local_mixer_gain = lax.dynamic_slice_in_dim(mixer_norm_gain, own_start, own_width)
    local_feedforward_gain = lax.dynamic_slice_in_dim(feedforward_norm_gain, own_start, own_width)
    input_half = block_input.reshape(tok_rows, own_width)
    local_input = input_half.astype(jnp.float32)
    upstream_gradient = out_grad.reshape(tok_rows, own_width)
    mask_list = same_masks(segment_ids)
    mixer_in, mixer_out = (
        lax.all_to_all(in_weight, "col", split_axis=2, concat_axis=1, tiled=True),
        lax.all_to_all(
            jnp.transpose(out_weight)[None], "col", split_axis=2, concat_axis=1, tiled=True
        ),
    )
    mixer_out = mixer_out[0]
    swiglu_gate, swiglu_up, swiglu_down = (
        lax.all_to_all(gate_weight, "col", split_axis=1, concat_axis=0, tiled=True),
        lax.all_to_all(up_weight, "col", split_axis=1, concat_axis=0, tiled=True),
        lax.all_to_all(jnp.transpose(down_weight), "col", split_axis=1, concat_axis=0, tiled=True),
    )
    complete_input = full_width(input_half).astype(jnp.float32)
    mixer_inverse_scale = full_scale(complete_input)
    mixer_normed = (complete_input * mixer_inverse_scale * mixer_norm_gain).astype(jnp.bfloat16)
    mixer_normalized = local_input * mixer_inverse_scale
    projected = jnp.einsum(
        "td,jdc->jtc", mixer_normed, mixer_in, preferred_element_type=jnp.float32
    )
    shaped = projected.reshape(3, seq_count, seq_length, own_width)
    b_proj, c_proj, x_proj = (shaped[0], shaped[1], shaped[2])
    mixed_in = b_proj * x_proj
    conved = conv_forward(mixed_in, mask_list, kernel)
    gated_out = (c_proj * conved).astype(jnp.bfloat16).reshape(tok_rows, own_width)
    mixer_partial = jnp.einsum(
        "tc,dc->td", gated_out, mixer_out, preferred_element_type=jnp.float32
    )
    resid_full = complete_input + summed_all(mixer_partial)
    feedforward_inverse_scale = full_scale(resid_full)
    feedforward_normed = (resid_full * feedforward_inverse_scale * feedforward_norm_gain).astype(
        jnp.bfloat16
    )
    local_residual = lax.dynamic_slice_in_dim(resid_full, own_start, own_width, axis=1)
    feedforward_normalized = local_residual * feedforward_inverse_scale
    gate_pre = jnp.dot(feedforward_normed, swiglu_gate, preferred_element_type=jnp.float32)
    up_pre = jnp.dot(feedforward_normed, swiglu_up, preferred_element_type=jnp.float32)
    sigmoid = jax.nn.sigmoid(gate_pre)
    activated = (gate_pre * sigmoid * up_pre).astype(jnp.bfloat16)
    swiglu_partial = jnp.einsum(
        "tf,df->td", activated, swiglu_down, preferred_element_type=jnp.float32
    )
    swiglu_full = summed_all(swiglu_partial)
    output_own = local_residual + lax.dynamic_slice_in_dim(
        swiglu_full, own_start, own_width, axis=1
    )
    cot_full = full_width(upstream_gradient)
    d_act = jnp.einsum("td,df->tf", cot_full, swiglu_down, preferred_element_type=jnp.float32)
    grad_down_piece = jnp.einsum(
        "td,tf->df", cot_full, activated, preferred_element_type=jnp.float32
    )
    d_up = (d_act * gate_pre * sigmoid).astype(jnp.bfloat16)
    d_gate = (d_act * up_pre * sigmoid * (1.0 + gate_pre * (1.0 - sigmoid))).astype(jnp.bfloat16)
    grad_gate_piece = jnp.einsum(
        "td,tf->df", feedforward_normed, d_gate, preferred_element_type=jnp.float32
    )
    grad_up_piece = jnp.einsum(
        "td,tf->df", feedforward_normed, d_up, preferred_element_type=jnp.float32
    )
    norm_two_partial = jnp.einsum(
        "tf,df->td", d_gate, swiglu_gate, preferred_element_type=jnp.float32
    ) + jnp.einsum("tf,df->td", d_up, swiglu_up, preferred_element_type=jnp.float32)
    grad_gate_w, grad_up_w, grad_down_t = (
        lax.all_to_all(
            grad_gate_piece.astype(jnp.bfloat16), "col", split_axis=0, concat_axis=1, tiled=True
        ).astype(grad_gate_piece.dtype),
        lax.all_to_all(
            grad_up_piece.astype(jnp.bfloat16), "col", split_axis=0, concat_axis=1, tiled=True
        ).astype(grad_up_piece.dtype),
        lax.all_to_all(
            grad_down_piece.astype(jnp.bfloat16), "col", split_axis=0, concat_axis=1, tiled=True
        ).astype(grad_down_piece.dtype),
    )
    grad_down_w = jnp.transpose(grad_down_t)
    feedforward_normed_gradient = own_share(norm_two_partial)
    feedforward_gain_gradient = jnp.sum(
        feedforward_normed_gradient * feedforward_normalized, axis=0
    )
    residual_gradient = upstream_gradient.astype(jnp.float32) + norm_reverse_result(
        feedforward_normed_gradient,
        feedforward_normalized,
        feedforward_inverse_scale,
        local_feedforward_gain,
    )
    resid_grad_full = full_width(residual_gradient.astype(jnp.bfloat16))
    grad_out_piece = jnp.einsum(
        "td,tc->dc", resid_grad_full, gated_out, preferred_element_type=jnp.float32
    )
    d_gated = jnp.einsum(
        "td,dc->tc", resid_grad_full, mixer_out, preferred_element_type=jnp.float32
    )
    d_gated = d_gated.reshape(seq_count, seq_length, own_width)
    d_cproj = (d_gated * conved).astype(jnp.bfloat16)
    d_conved = d_gated * c_proj
    d_mixed, grad_kernel = conv_backward(d_conved, mixed_in, mask_list, kernel)
    d_bproj = (d_mixed * x_proj).astype(jnp.bfloat16)
    d_xproj = (d_mixed * b_proj).astype(jnp.bfloat16)
    d_projected = jnp.stack([d_bproj, d_cproj, d_xproj]).reshape(3, tok_rows, own_width)
    grad_in_piece = jnp.einsum(
        "td,jtc->jdc", mixer_normed, d_projected, preferred_element_type=jnp.float32
    )
    norm_one_partial = jnp.einsum(
        "jtc,jdc->td", d_projected, mixer_in, preferred_element_type=jnp.float32
    )
    grad_in_w, grad_out_t = (
        lax.all_to_all(
            grad_in_piece.astype(jnp.bfloat16), "col", split_axis=1, concat_axis=2, tiled=True
        ).astype(grad_in_piece.dtype),
        lax.all_to_all(
            grad_out_piece[None].astype(jnp.bfloat16),
            "col",
            split_axis=1,
            concat_axis=2,
            tiled=True,
        ).astype(jnp.float32),
    )
    grad_out_w = jnp.transpose(grad_out_t[0])
    mixer_normed_gradient = own_share(norm_one_partial)
    mixer_gain_gradient = jnp.sum(mixer_normed_gradient * mixer_normalized, axis=0)
    block_input_gradient = residual_gradient + norm_reverse_result(
        mixer_normed_gradient, mixer_normalized, mixer_inverse_scale, local_mixer_gain
    )
    (
        in_total,
        out_total,
        gate_total,
        up_total,
        down_total,
        kernel_total,
        gain_one_total,
        gain_two_total,
    ) = (
        lax.psum(grad_in_w.astype(jnp.bfloat16), "dp").astype(jnp.float32),
        lax.psum(grad_out_w.astype(jnp.bfloat16), "dp").astype(jnp.float32),
        lax.psum(grad_gate_w.astype(jnp.bfloat16), "dp").astype(jnp.float32),
        lax.psum(grad_up_w.astype(jnp.bfloat16), "dp").astype(jnp.float32),
        lax.psum(grad_down_w.astype(jnp.bfloat16), "dp").astype(jnp.float32),
        lax.psum(grad_kernel.astype(jnp.bfloat16), "dp").astype(jnp.float32),
        lax.psum(mixer_gain_gradient.astype(jnp.bfloat16), "dp").astype(jnp.float32),
        lax.psum(feedforward_gain_gradient.astype(jnp.bfloat16), "dp").astype(jnp.float32),
    )
    block_output = output_own.astype(jnp.bfloat16).reshape(seq_count, seq_length, own_width)
    return (
        block_output,
        block_input_gradient.reshape(seq_count, seq_length, own_width),
        in_total,
        out_total,
        gate_total,
        up_total,
        down_total,
        kernel_total,
        gain_one_total,
        gain_two_total,
    )


def solution(mesh):
    placed = (
        P("dp", None, ("row", "col")),
        P("dp", None),
        P("dp", None, ("row", "col")),
        P(None, "col", "row"),
        P("row", "col"),
        P("col", "row"),
        P("col", "row"),
        P("row", "col"),
        P(None, ("row", "col")),
        P(),
        P(),
    )
    return jax.shard_map(
        body,
        mesh=mesh,
        in_specs=placed,
        out_specs=(
            P("dp", None, ("row", "col")),
            P("dp", None, ("row", "col")),
            P(None, "col", "row"),
            P("row", "col"),
            P("col", "row"),
            P("col", "row"),
            P("row", "col"),
            P(None, ("row", "col")),
            P(("row", "col")),
            P(("row", "col")),
        ),
        check_vma=False,
    )
```

profile of v0, /device:TPU:0, one launch (start us, length us, event | category | flops | bytes accessed | tf_op | source)
XLA Modules:
  0.0 1171.5 jit_solution(15314142527145957673)
XLA Ops:
  28.1 16.2 %all-to-all-done = bf16[3,512,256]{1,0,2:T(4,128)(2,1)S(1)} async-done(((bf16[3,512,256]{1,0,2:T(4,128)(2,1)}), bf16[3,512,256]{1,0,2:T(4,128)(2,1)S(1)}, u32[]{:S(2)}, u32[]{:S(2)}) %all-to-all-start) | async-done | bytes 786464 | tf_op jit(solution)/shard_map/all_to_all | solution.py:104
  45.1 22.4 %all-gather.4.cloned.1.call-done = bf16[3584,1024]{1,0:T(8,128)(2,1)} async-done(((bf16[3584,128]{1,0:T(8,128)(2,1)}), bf16[3584,1024]{1,0:T(8,128)(2,1)}) %all-gather.4.cloned.1.call-update) | async-done | bytes 7340048 | tf_op jit(solution)/shard_map/all_gather | solution.py:55
  99.2 26.4 %all-to-all-done.2 = bf16[512,2,576]{0,2,1:T(8,128)(2,1)S(1)} async-done(((bf16[512,2,576]{0,2,1:T(8,128)(2,1)}), bf16[512,2,576]{0,2,1:T(8,128)(2,1)S(1)}, u32[]{:S(2)}, u32[]{:S(2)}) %all-to-all-start.2) | async-done | bytes 1179680 | tf_op jit(solution)/shard_map/all_to_all | solution.py:111
  125.6 33.1 %all_to_all.168 = bf16[512,2,576]{0,2,1:T(8,128)(2,1)} all-to-all(bf16[512,2,576]{0,2,1:T(8,128)(2,1)} %bitcast.166), channel_id=1, replica_groups=mesh['dp'=4,'row'=4,'col'=2] {'col'}, dimensions={1} | all-to-all | bytes 2359296 | tf_op jit(solution)/shard_map/all_to_all | solution.py:112
  166.3 25.3 %all-to-all-done.4 = bf16[512,2,576]{0,2,1:T(8,128)(2,1)} async-done(((bf16[512,2,576]{0,2,1:T(8,128)(2,1)}), bf16[512,2,576]{0,2,1:T(8,128)(2,1)}, u32[]{:S(2)}, u32[]{:S(2)}) %all-to-all-start.4) | async-done | bytes 1179680 | tf_op jit(solution)/shard_map/all_to_all | solution.py:113
  193.1 130.1 %all-reduce.12.cloned.1.call-done = f32[3584,1024]{1,0:T(8,128)} async-done(((f32[3584,1024]{1,0:T(8,128)}), f32[3584,1024]{1,0:T(8,128)}) %all-reduce.12.cloned.1.call-update) | async-done | bytes 14680080 | tf_op jit(solution)/shard_map/psum | solution.py:63
  323.2 13.8 %multiply_reduce_fusion = (f32[3584]{0:T(1024)S(1)}, f32[3584,1024]{1,0:T(8,128)}) fusion(f32[3584,1024]{1,0:T(8,128)} %all-reduce.12.cloned.1.call-done, bf16[3584,1024]{1,0:T(8,128)(2,1)} %all-gather.4.cloned.1.call-done), kind=kLoop, calls=%fused_computation.7 | loop fusion | flops 14676480 | bytes 36714496 | tf_op jit(solution)/shard_map/reduce_sum | solution.py:71
  337.0 9.4 multiply_convert_fusion
  346.4 11.2 fusion.19
  364.3 12.2 %all-gather.6.cloned.1.call-done = bf16[3584,1024]{1,0:T(8,128)(2,1)} async-done(((bf16[3584,128]{1,0:T(8,128)(2,1)}), bf16[3584,1024]{1,0:T(8,128)(2,1)}) %all-gather.6.cloned.1.call-update) | async-done | bytes 7340048 | tf_op jit(solution)/shard_map/all_gather | solution.py:55
  376.5 15.9 %multiply_convert_fusion.1 = (bf16[3584,576]{0,1:T(8,128)(2,1)S(1)}, bf16[3584,576]{0,1:T(8,128)(2,1)S(1)}, bf16[3584,576]{0,1:T(8,128)(2,1)}) fusion(f32[3584,576]{0,1:T(8,128)} %fusion.19, f32[3584,576]{0,1:T(8,128)} %fusion.20, bf16[3584,1024]{1,0:T(8,128)(2,1)} %all-gather.6.cloned.1.call-done, bf16[1024,576]{0,1:T(8,128)(2,1)S(1)} %bitcast.187), kind=kOutput, calls=%fused_computation.9 | convolution fusion | flops 4260888576 | bytes 37421056 | tf_op jit(solution)/shard_map/td,df->tf/dot_general | solution.py:149
  392.4 9.6 fusion.22
  402.0 12.3 %convolution_add_fusion = f32[3584,1024]{1,0:T(8,128)} fusion(f32[3584,1024]{1,0:T(8,128)} %fusion.22, bf16[3584,576]{0,1:T(8,128)(2,1)S(1)} %get-tuple-element.74, bf16[1024,576]{0,1:T(8,128)(2,1)S(1)} %bitcast.192), kind=kOutput, calls=%fused_computation.13 | convolution fusion | flops 4231528448 | bytes 34668544 | tf_op jit(solution)/shard_map/tf,df->td/dot_general | solution.py:163
  414.4 102.2 %reduce-scatter.3.cloned.1.call-done = f32[3584,128]{1,0:T(8,128)} async-done(((f32[3584,1024]{1,0:T(8,128)}), f32[3584,128]{1,0:T(8,128)}) %reduce-scatter.3.cloned.1.call-update) | async-done | bytes 1835024 | tf_op jit(solution)/shard_map/reduce_scatter | solution.py:59
  520.7 23.8 %psum.86 = f32[3584]{0:T(1024)S(1)} all-reduce(f32[3584]{0:T(1024)S(1)} %get-tuple-element.51), channel_id=1, replica_groups=mesh['dp'=4,'row'=4,'col'=2] {'row','col'}, use_global_device_ids=true, to_apply=%region_6.7 | all-reduce | flops 3584 | bytes 28672 | tf_op jit(solution)/shard_map/psum | solution.py:67
  548.9 8.8 convolution_convert_fusion.1
  572.4 32.6 %all-gather.8.cloned.1.call-done = bf16[3584,1024]{1,0:T(8,128)(2,1)} async-done(((bf16[3584,128]{1,0:T(8,128)(2,1)}), bf16[3584,1024]{1,0:T(8,128)(2,1)}) %all-gather.8.cloned.1.call-update) | async-done | bytes 7340048 | tf_op jit(solution)/shard_map/all_gather | solution.py:55
  687.0 10.6 convolution_bitcast_fusion
  698.9 11.3 fusion.21
  711.4 142.0 %all-reduce.16.cloned.1.call-done = (bf16[512,1152]{0,1:T(8,128)(2,1)}, bf16[512,1152]{0,1:T(8,128)(2,1)}, bf16[3,512,256]{2,1,0:T(8,128)(2,1)}, bf16[256,512]{1,0:T(8,128)(2,1)}, bf16[1152,512]{1,0:T(8,128)(2,1)}) async-done(((bf16[512,1152]{0,1:T(8,128)(2,1)}, bf16[512,1152]{0,1:T(8,128)(2,1)}, bf16[3,512,256]{2,1,0:T(8,128)(2,1)}, bf16[256,512]{1,0:T(8,128)(2,1)}, bf16[1152,512]{1,0:T(8,128)(2,1)}), ...) | async-done | bytes 4587536 | tf_op jit(solution)/shard_map/psum | solution.py:236
  862.2 95.9 %reduce-scatter.5.cloned.1.call-done = f32[3584,128]{1,0:T(8,128)} async-done(((f32[3584,1024]{1,0:T(8,128)}), f32[3584,128]{1,0:T(8,128)}) %reduce-scatter.5.cloned.1.call-update) | async-done | bytes 1835024 | tf_op jit(solution)/shard_map/reduce_scatter | solution.py:59
  961.1 11.7 all-reduce.6
  974.5 25.8 %psum.87 = f32[3584]{0:T(1024)S(1)} all-reduce(f32[3584]{0:T(1024)S(1)} %get-tuple-element.53), channel_id=1, replica_groups=mesh['dp'=4,'row'=4,'col'=2] {'row','col'}, use_global_device_ids=true, to_apply=%region_9.10 | all-reduce | flops 3584 | bytes 28672 | tf_op jit(solution)/shard_map/psum | solution.py:67
  1000.2 157.4 %all-reduce.14.cloned.1.call-done = f32[3584,1024]{1,0:T(8,128)} async-done(((f32[3584,1024]{1,0:T(8,128)}), f32[3584,1024]{1,0:T(8,128)}) %all-reduce.14.cloned.1.call-update) | async-done | bytes 14680080 | tf_op jit(solution)/shard_map/psum | solution.py:63
  (195 shorter events, 196.6 us)
Async XLA Ops:
  7.2 60.3 %all-gather.4.cloned.1.call-start = ((), (), s32[]{:S(2)}) async-start(), calls=%async_computation.12 | async-start | bytes 8257536 | tf_op jit(solution)/shard_map/all_gather | solution.py:55
  13.1 10.5 all-to-all-start.1
  23.6 20.7 %all-to-all-start = ((bf16[3,512,256]{1,0,2:T(4,128)(2,1)}), bf16[3,512,256]{1,0,2:T(4,128)(2,1)S(1)}, u32[]{:S(2)}, u32[]{:S(2)}) async-start(bf16[3,512,256]{1,0,2:T(4,128)(2,1)} %copy.81), calls=%async_computation | async-start | bytes 2097152 | tf_op jit(solution)/shard_map/all_to_all | solution.py:104
  27.2 296.0 %all-reduce.12.cloned.1.call-start = ((), (), s32[]{:S(2)}) async-start(), calls=%async_computation.13 | async-start | bytes 29360128 | tf_op jit(solution)/shard_map/psum | solution.py:63
  90.3 286.1 %all-gather.6.cloned.1.call-start = ((), (), s32[]{:S(2)}) async-start(), calls=%async_computation.15 | async-start | bytes 8257536 | tf_op jit(solution)/shard_map/all_gather | solution.py:55
  93.0 32.6 %all-to-all-start.2 = ((bf16[512,2,576]{0,2,1:T(8,128)(2,1)}), bf16[512,2,576]{0,2,1:T(8,128)(2,1)S(1)}, u32[]{:S(2)}, u32[]{:S(2)}) async-start(bf16[512,2,576]{0,2,1:T(8,128)(2,1)} %bitcast.165), calls=%async_computation.2 | async-start | bytes 2359296 | tf_op jit(solution)/shard_map/all_to_all | solution.py:111
  158.7 33.0 %all-to-all-start.4 = ((bf16[512,2,576]{0,2,1:T(8,128)(2,1)}), bf16[512,2,576]{0,2,1:T(8,128)(2,1)}, u32[]{:S(2)}, u32[]{:S(2)}) async-start(bf16[512,2,576]{0,2,1:T(8,128)(2,1)} %bitcast.186), calls=%async_computation.4 | async-start | bytes 2359296 | tf_op jit(solution)/shard_map/all_to_all | solution.py:113
  163.1 353.5 %reduce-scatter.3.cloned.1.call-start = ((), (), s32[]{:S(2)}) async-start(), calls=%async_computation.16 | async-start | bytes 16515072 | tf_op jit(solution)/shard_map/reduce_scatter | solution.py:59
  193.0 183.4 %copy-start.21 = (bf16[2,72,8,512]{3,2,0,1:T(8,128)(2,1)}, bf16[2,72,8,512]{3,2,0,1:T(8,128)(2,1)S(1)}, u32[]{:S(2)}) copy-start(bf16[2,72,8,512]{3,2,0,1:T(8,128)(2,1)S(1)} %copy.109) | copy-start | bytes 3538948
  193.1 143.9 %copy-start.38 = (f32[1024]{0:T(1024)S(1)}, f32[1024]{0:T(1024)}, u32[]{:S(2)}) copy-start(f32[1024]{0:T(1024)} %param.21) | copy-start | bytes 12292
  414.3 190.8 %all-gather.8.cloned.1.call-start = ((), (), s32[]{:S(2)}) async-start(), calls=%async_computation.17 | async-start | bytes 8257536 | tf_op jit(solution)/shard_map/all_gather | solution.py:55
  558.7 59.6 %all-to-all-start.7 = ((bf16[2,512,576]{1,2,0:T(8,128)(2,1)}), bf16[2,512,576]{1,2,0:T(8,128)(2,1)S(1)}, u32[]{:S(2)}, u32[]{:S(2)}) async-start(bf16[2,512,576]{1,2,0:T(8,128)(2,1)} %bitcast.162), calls=%async_computation.9 | async-start | bytes 2359296 | tf_op jit(solution)/shard_map/all_to_all | solution.py:165
  618.3 20.4 %all-to-all-start.8 = ((bf16[2,512,576]{1,2,0:T(8,128)(2,1)}), bf16[2,512,576]{1,2,0:T(8,128)(2,1)}, u32[]{:S(2)}, u32[]{:S(2)}) async-start(bf16[2,512,576]{1,2,0:T(8,128)(2,1)} %bitcast.140), calls=%async_computation.10 | async-start | bytes 2359296 | tf_op jit(solution)/shard_map/all_to_all | solution.py:168
  638.7 12.0 %all-to-all-start.6 = ((bf16[2,2,32768]{2,1,0:T(2,128)(2,1)}), bf16[2,2,32768]{2,1,0:T(2,128)(2,1)S(1)}, u32[]{:S(2)}, u32[]{:S(2)}) async-start(bf16[2,2,32768]{2,1,0:T(2,128)(2,1)} %reshape.120), calls=%async_computation.8 | async-start | bytes 524288 | tf_op jit(solution)/shard_map/all_to_all | solution.py:210
  650.8 17.0 %all-to-all-start.5 = ((bf16[3,1024,128]{2,0,1:T(4,128)(2,1)}), bf16[3,1024,128]{2,0,1:T(4,128)(2,1)S(1)}, u32[]{:S(2)}, u32[]{:S(2)}) async-start(bf16[3,1024,128]{2,0,1:T(4,128)(2,1)} %copy.92), calls=%async_computation.7 | async-start | bytes 2097152 | tf_op jit(solution)/shard_map/all_to_all | solution.py:207
  667.8 17.6 %all-to-all-start.9 = ((bf16[2,512,576]{1,2,0:T(8,128)(2,1)}), bf16[2,512,576]{1,2,0:T(8,128)(2,1)S(1)}, u32[]{:S(2)}, u32[]{:S(2)}) async-start(bf16[2,512,576]{1,2,0:T(8,128)(2,1)} %bitcast.139), calls=%async_computation.11 | async-start | bytes 2359296 | tf_op jit(solution)/shard_map/all_to_all | solution.py:171
  671.4 182.0 %all-reduce.16.cloned.1.call-start = ((), (), s32[]{:S(2)}) async-start(), calls=%async_computation.19 | async-start | bytes 9175040 | tf_op jit(solution)/shard_map/psum | solution.py:236
  686.4 271.7 %reduce-scatter.5.cloned.1.call-start = ((), (), s32[]{:S(2)}) async-start(), calls=%async_computation.18 | async-start | bytes 16515072 | tf_op jit(solution)/shard_map/reduce_scatter | solution.py:59
  697.6 460.0 %all-reduce.14.cloned.1.call-start = ((), (), s32[]{:S(2)}) async-start(), calls=%async_computation.14 | async-start | bytes 29360128 | tf_op jit(solution)/shard_map/psum | solution.py:63
  861.3 296.3 %copy-start.1 = (f32[3584,128]{1,0:T(8,128)S(1)}, f32[3584,128]{1,0:T(8,128)}, u32[]{:S(2)}) copy-start(f32[3584,128]{1,0:T(8,128)} %reduce-scatter.3.cloned.1.call-done) | copy-start | bytes 5505028
  861.3 296.3 %copy-start.31 = (f32[3584]{0:T(1024)S(1)}, f32[3584]{0:T(1024)}, u32[]{:S(2)}) copy-start(f32[3584]{0:T(1024)} %copy-done.29) | copy-start | bytes 43012
  861.3 296.3 %copy-start.33 = (f32[3584]{0:T(1024)S(1)}, f32[3584]{0:T(1024)}, u32[]{:S(2)}) copy-start(f32[3584]{0:T(1024)} %copy-done.32) | copy-start | bytes 43012
  861.3 296.3 %copy-start.36 = (f32[128]{0:T(128)S(1)}, f32[128]{0:T(128)}, u32[]{:S(2)}) copy-start(f32[128]{0:T(128)} %copy-done.35) | copy-start | bytes 1540
  861.3 296.3 %copy-start.40 = (f32[128]{0:T(128)S(1)}, f32[128]{0:T(128)}, u32[]{:S(2)}) copy-start(f32[128]{0:T(128)} %dynamic_slice.15) | copy-start | bytes 1540
  (42 other events, 797.5 us)
Sparse Core Ops, SparseCore 0:
  9.9 57.6 all-gather.3
  90.4 232.7 all-reduce.11
  325.1 51.3 all-gather.5
  414.4 102.1 reduce-scatter.2
  549.0 56.0 all-gather.7
  686.5 166.8 all-reduce.15
  856.9 101.1 reduce-scatter.4
  961.6 196.0 all-reduce.13
where the time goes:
time: 1180 us; the launch traced here: 1170 us
  waiting for transfers between devices  783 us (66%)
  matrix products  135 us (11%)
  blocking collectives  94.4 us (8%)
  other arithmetic  67.4 us (6%)
  local copies, waits for them, and re-layouts  40.8 us (3%)
  starting transfers between devices  36.2 us (3%)
  between operations  15 us (1%)
    psum x2, waiting for transfers between devices, summed_all(): return lax.psum(partial_sum, ('row', 'col'))  288 us
    reduce_scatter x2, waiting for transfers between devices, own_share(): lax.psum_scatter(partial_sum, ('row', 'col'), scatter_dimension=1, tiled=...  198 us
    psum x1, waiting for transfers between devices, body(): lax.psum(grad_gate_w.astype(jnp.bfloat16), 'dp').astype(jnp.float32)  142 us
    all_gather x3, waiting for transfers between devices, full_width(): return lax.all_gather(part_half, ('row', 'col'), axis=1, tiled=True)  67.3 us
    psum x2, blocking collectives, token_stat(): return lax.psum(jnp.sum(values, axis=1), ('row', 'col'))  49.6 us
    all_to_all x1, blocking collectives, body(): lax.all_to_all(up_weight, 'col', split_axis=1, concat_axis=0, tiled=True)  33.1 us
    all_to_all x1, waiting for transfers between devices, body(): lax.all_to_all(gate_weight, 'col', split_axis=1, concat_axis=0, tiled=True)  26.4 us
    all_to_all x1, waiting for transfers between devices, body(): lax.all_to_all(jnp.transpose(down_weight), 'col', split_axis=1, concat_ax...  25.3 us
  transfers between devices with their start and end apart: 17, of which 15 were waited for; matrix products, arithmetic and copies ran while one was open for 14% of the time, Pallas kernels for 0%

commit v1 on v0

--- a/solution.py
+++ b/solution.py
@@ -60,7 +60,7 @@
 
 
 def summed_all(partial_sum):
-    return lax.psum(partial_sum, ("row", "col"))
+    return jnp.sum(lax.all_gather(partial_sum, ("row", "col")), axis=0)
 
 
 def token_stat(values):

time: 1180 us -> 1870 us (1.58)
  waiting for transfers between devices: 783 us -> 1400 us
  other arithmetic: 67.4 us -> 152 us
    all_gather x0 -> x2, waiting for transfers between devices: none -> 932 us  [summed_all(): return jnp.sum(lax.all_gather(partial_sum, ('row', 'col')), axis=0)]
    psum x2 -> x0, waiting for transfers between devices: 288 us -> none  [summed_all(): return lax.psum(partial_sum, ('row', 'col'))]
    reduce_sum x0 -> x2, other arithmetic: none -> 85.4 us  [summed_all(): return jnp.sum(lax.all_gather(partial_sum, ('row', 'col')), axis=0)]
  transfers between devices with their start and end apart: 17 -> 17, of which waited for: 15 -> 14; matrix products, arithmetic and copies ran while one was open for 14% -> 11% of each run, Pallas kernels for 0% -> 0%
where the time goes in v1:
time: 1870 us
  waiting for transfers between devices  1400 us (75%)
  other arithmetic  152 us (8%)
  matrix products  133 us (7%)
  blocking collectives  91.1 us (5%)
  local copies, waits for them, and re-layouts  38.1 us (2%)
  starting transfers between devices  35 us (2%)
    all_gather x2, waiting for transfers between devices, summed_all(): return jnp.sum(lax.all_gather(partial_sum, ('row', 'col')), axis=0)  932 us
    reduce_scatter x2, waiting for transfers between devices, own_share(): lax.psum_scatter(partial_sum, ('row', 'col'), scatter_dimension=1, tiled=...  197 us
    psum x1, waiting for transfers between devices, body(): lax.psum(grad_gate_w.astype(jnp.bfloat16), 'dp').astype(jnp.float32)  142 us
    reduce_sum x2, other arithmetic, summed_all(): return jnp.sum(lax.all_gather(partial_sum, ('row', 'col')), axis=0)  85.4 us
    all_gather x3, waiting for transfers between devices, full_width(): return lax.all_gather(part_half, ('row', 'col'), axis=1, tiled=True)  55 us
    psum x2, blocking collectives, token_stat(): return lax.psum(jnp.sum(values, axis=1), ('row', 'col'))  48.6 us
  transfers between devices with their start and end apart: 17, of which 14 were waited for; matrix products, arithmetic and copies ran while one was open for 11% of the time, Pallas kernels for 0%

profile of v1, /device:TPU:0, one launch (start us, length us, event | category | flops | bytes accessed | tf_op | source)
XLA Modules:
  0.0 1867.2 jit_solution(11339634559872991774)
XLA Ops:
  28.1 16.2 all-to-all-done
  45.1 22.4 %all-gather.8.cloned.1.call-done = bf16[3584,1024]{1,0:T(8,128)(2,1)} async-done(((bf16[3584,128]{1,0:T(8,128)(2,1)}), bf16[3584,1024]{1,0:T(8,128)(2,1)}) %all-gather.8.cloned.1.call-update) | async-done | bytes 7340048 | tf_op jit(solution)/shard_map/all_gather | solution.py:55
  97.4 15.1 all-to-all-done.2
  112.4 30.8 %all_to_all.168 = bf16[512,2,576]{0,2,1:T(8,128)(2,1)S(1)} all-to-all(bf16[512,2,576]{0,2,1:T(8,128)(2,1)S(1)} %bitcast.167), channel_id=1, replica_groups=mesh['dp'=4,'row'=4,'col'=2] {'col'}, dimensions={1} | all-to-all | bytes 2359296 | tf_op jit(solution)/shard_map/all_to_all | solution.py:112
  149.3 25.7 %all-to-all-done.4 = bf16[512,2,576]{0,2,1:T(8,128)(2,1)S(1)} async-done(((bf16[512,2,576]{0,2,1:T(8,128)(2,1)}), bf16[512,2,576]{0,2,1:T(8,128)(2,1)S(1)}, u32[]{:S(2)}, u32[]{:S(2)}) %all-to-all-start.4) | async-done | bytes 1179680 | tf_op jit(solution)/shard_map/all_to_all | solution.py:113
  175.3 455.0 %all-gather.14.cloned.1.call-done = f32[28672,1024]{1,0:T(8,128)} async-done(((f32[3584,1024]{1,0:T(8,128)}), f32[28672,1024]{1,0:T(8,128)}) %all-gather.14.cloned.1.call-update) | async-done | bytes 117440528 | tf_op jit(solution)/shard_map/all_gather | solution.py:63
  630.2 43.7 %reduce_sum.100 = f32[3584,1024]{1,0:T(8,128)} reduce(f32[8,3584,1024]{2,1,0:T(8,128)} %bitcast.17, f32[]{:T(128)} %constant.11.clone.1), dimensions={0}, to_apply=%region_1.2 | reduce | flops 25690112 | bytes 132120576 | tf_op jit(solution)/shard_map/reduce_sum | solution.py:63
  674.0 12.6 multiply_reduce_fusion
  686.6 9.4 multiply_convert_fusion
  696.1 9.9 fusion.19
  712.7 17.4 multiply_convert_fusion.1
  737.9 11.9 convolution_add_fusion
  750.6 101.5 %reduce-scatter.3.cloned.1.call-done = f32[3584,128]{1,0:T(8,128)} async-done(((f32[3584,1024]{1,0:T(8,128)}), f32[3584,128]{1,0:T(8,128)}) %reduce-scatter.3.cloned.1.call-update) | async-done | bytes 1835024 | tf_op jit(solution)/shard_map/reduce_scatter | solution.py:59
  856.4 23.8 %psum.70 = f32[3584]{0:T(1024)S(1)} all-reduce(f32[3584]{0:T(1024)S(1)} %get-tuple-element.51), channel_id=1, replica_groups=mesh['dp'=4,'row'=4,'col'=2] {'row','col'}, use_global_device_ids=true, to_apply=%region_6.7 | all-reduce | flops 3584 | bytes 28672 | tf_op jit(solution)/shard_map/psum | solution.py:67
  907.9 32.6 %all-gather.12.cloned.1.call-done = bf16[3584,1024]{1,0:T(8,128)(2,1)} async-done(((bf16[3584,128]{1,0:T(8,128)(2,1)}), bf16[3584,1024]{1,0:T(8,128)(2,1)}) %all-gather.12.cloned.1.call-update) | async-done | bytes 7340048 | tf_op jit(solution)/shard_map/all_gather | solution.py:55
  989.8 8.8 convolution_convert_fusion.2
  1022.4 10.6 convolution_bitcast_fusion
  1034.2 11.3 fusion.21
  1046.7 142.1 %all-reduce.10.cloned.1.call-done = (bf16[512,1152]{0,1:T(8,128)(2,1)}, bf16[512,1152]{0,1:T(8,128)(2,1)}, bf16[3,512,256]{2,1,0:T(8,128)(2,1)}, bf16[256,512]{1,0:T(8,128)(2,1)}, bf16[1152,512]{1,0:T(8,128)(2,1)}) async-done(((bf16[512,1152]{0,1:T(8,128)(2,1)}, bf16[512,1152]{0,1:T(8,128)(2,1)}, bf16[3,512,256]{2,1,0:T(8,128)(2,1)}, bf16[256,512]{1,0:T(8,128)(2,1)}, bf16[1152,512]{1,0:T(8,128)(2,1)}), ...) | async-done | bytes 4587536 | tf_op jit(solution)/shard_map/psum | solution.py:236
  1197.5 95.9 %reduce-scatter.5.cloned.1.call-done = f32[3584,128]{1,0:T(8,128)} async-done(((f32[3584,1024]{1,0:T(8,128)}), f32[3584,128]{1,0:T(8,128)}) %reduce-scatter.5.cloned.1.call-update) | async-done | bytes 1835024 | tf_op jit(solution)/shard_map/reduce_scatter | solution.py:59
  1296.8 11.7 all-reduce.6
  1310.1 24.8 %psum.71 = f32[3584]{0:T(1024)S(1)} all-reduce(f32[3584]{0:T(1024)S(1)} %get-tuple-element.53), channel_id=1, replica_groups=mesh['dp'=4,'row'=4,'col'=2] {'row','col'}, use_global_device_ids=true, to_apply=%region_9.10 | all-reduce | flops 3584 | bytes 28672 | tf_op jit(solution)/shard_map/psum | solution.py:67
  1334.9 476.8 %all-gather.16.cloned.1.call-done = f32[28672,1024]{1,0:T(8,128)} async-done(((f32[3584,1024]{1,0:T(8,128)}), f32[28672,1024]{1,0:T(8,128)}) %all-gather.16.cloned.1.call-update) | async-done | bytes 117440528 | tf_op jit(solution)/shard_map/all_gather | solution.py:63
  1811.7 41.7 %reduce_sum.102 = f32[3584,1024]{1,0:T(8,128)} reduce(f32[8,3584,1024]{2,1,0:T(8,128)} %bitcast.25, f32[]{:T(128)} %constant.11.clone.1), dimensions={0}, to_apply=%region_3.4 | reduce | flops 25690112 | bytes 132120576 | tf_op jit(solution)/shard_map/reduce_sum | solution.py:63
  (225 shorter events, 200.5 us)
Async XLA Ops:
  7.2 60.3 %all-gather.8.cloned.1.call-start = ((), (), s32[]{:S(2)}) async-start(), calls=%async_computation.12 | async-start | bytes 8257536 | tf_op jit(solution)/shard_map/all_gather | solution.py:55
  13.1 10.5 all-to-all-start.1
  23.6 20.7 %all-to-all-start = ((bf16[3,512,256]{1,0,2:T(4,128)(2,1)}), bf16[3,512,256]{1,0,2:T(4,128)(2,1)S(1)}, u32[]{:S(2)}, u32[]{:S(2)}) async-start(bf16[3,512,256]{1,0,2:T(4,128)(2,1)} %copy.81), calls=%async_computation | async-start | bytes 2097152 | tf_op jit(solution)/shard_map/all_to_all | solution.py:104
  27.2 603.0 %all-gather.14.cloned.1.call-start = ((), (), s32[]{:S(2)}) async-start(), calls=%async_computation.17 | async-start | bytes 132120576 | tf_op jit(solution)/shard_map/all_gather | solution.py:63
  90.5 622.2 %all-gather.10.cloned.1.call-start = ((), (), s32[]{:S(2)}) async-start(), calls=%async_computation.13 | async-start | bytes 8257536 | tf_op jit(solution)/shard_map/all_gather | solution.py:55
  93.1 19.3 %all-to-all-start.2 = ((bf16[512,2,576]{0,2,1:T(8,128)(2,1)}), bf16[512,2,576]{0,2,1:T(8,128)(2,1)S(1)}, u32[]{:S(2)}, u32[]{:S(2)}) async-start(bf16[512,2,576]{0,2,1:T(8,128)(2,1)} %bitcast.18), calls=%async_computation.2 | async-start | bytes 2359296 | tf_op jit(solution)/shard_map/all_to_all | solution.py:111
  143.3 31.8 %all-to-all-start.4 = ((bf16[512,2,576]{0,2,1:T(8,128)(2,1)}), bf16[512,2,576]{0,2,1:T(8,128)(2,1)S(1)}, u32[]{:S(2)}, u32[]{:S(2)}) async-start(bf16[512,2,576]{0,2,1:T(8,128)(2,1)} %bitcast.187), calls=%async_computation.4 | async-start | bytes 2359296 | tf_op jit(solution)/shard_map/all_to_all | solution.py:113
  146.9 705.3 %reduce-scatter.3.cloned.1.call-start = ((), (), s32[]{:S(2)}) async-start(), calls=%async_computation.14 | async-start | bytes 16515072 | tf_op jit(solution)/shard_map/reduce_scatter | solution.py:59
  175.2 537.5 %copy-start.26 = (bf16[2,72,8,512]{3,2,0,1:T(8,128)(2,1)}, bf16[2,72,8,512]{3,2,0,1:T(8,128)(2,1)S(1)}, u32[]{:S(2)}) copy-start(bf16[2,72,8,512]{3,2,0,1:T(8,128)(2,1)S(1)} %copy.109) | copy-start | bytes 3538948
  749.8 190.6 %all-gather.12.cloned.1.call-start = ((), (), s32[]{:S(2)}) async-start(), calls=%async_computation.15 | async-start | bytes 8257536 | tf_op jit(solution)/shard_map/all_gather | solution.py:55
  750.6 129.6 %copy-start.44 = (f32[128]{0:T(128)}, f32[128]{0:T(128)S(1)}, u32[]{:S(2)}) copy-start(f32[128]{0:T(128)S(1)} %dynamic_slice.14) | copy-start | bytes 1540
  750.6 129.6 %copy-start.11 = (bf16[2,1792,128]{2,1,0:T(8,128)(2,1)S(1)}, bf16[2,1792,128]{2,1,0:T(8,128)(2,1)}, u32[]{:S(2)}) copy-start(bf16[2,1792,128]{2,1,0:T(8,128)(2,1)} %param.13) | copy-start | bytes 2752516
  894.1 59.6 %all-to-all-start.7 = ((bf16[2,512,576]{1,2,0:T(8,128)(2,1)}), bf16[2,512,576]{1,2,0:T(8,128)(2,1)S(1)}, u32[]{:S(2)}, u32[]{:S(2)}) async-start(bf16[2,512,576]{1,2,0:T(8,128)(2,1)} %bitcast.143), calls=%async_computation.9 | async-start | bytes 2359296 | tf_op jit(solution)/shard_map/all_to_all | solution.py:165
  953.7 20.4 %all-to-all-start.8 = ((bf16[2,512,576]{1,2,0:T(8,128)(2,1)}), bf16[2,512,576]{1,2,0:T(8,128)(2,1)}, u32[]{:S(2)}, u32[]{:S(2)}) async-start(bf16[2,512,576]{1,2,0:T(8,128)(2,1)} %bitcast.142), calls=%async_computation.10 | async-start | bytes 2359296 | tf_op jit(solution)/shard_map/all_to_all | solution.py:168
  974.1 12.0 all-to-all-start.6
  986.2 17.0 all-to-all-start.5
  1003.2 17.6 all-to-all-start.9
  1006.8 182.0 %all-reduce.10.cloned.1.call-start = ((), (), s32[]{:S(2)}) async-start(), calls=%async_computation.19 | async-start | bytes 9175040 | tf_op jit(solution)/shard_map/psum | solution.py:236
  1021.8 271.7 %reduce-scatter.5.cloned.1.call-start = ((), (), s32[]{:S(2)}) async-start(), calls=%async_computation.16 | async-start | bytes 16515072 | tf_op jit(solution)/shard_map/reduce_scatter | solution.py:59
  1033.0 778.7 %all-gather.16.cloned.1.call-start = ((), (), s32[]{:S(2)}) async-start(), calls=%async_computation.18 | async-start | bytes 132120576 | tf_op jit(solution)/shard_map/all_gather | solution.py:63
  1195.4 98.1 %copy-start.35 = (f32[3584]{0:T(1024)S(1)}, f32[3584]{0:T(1024)}, u32[]{:S(2)}) copy-start(f32[3584]{0:T(1024)} %copy-done.33) | copy-start | bytes 43012
  1195.4 98.1 %copy-start.55 = (f32[128]{0:T(128)S(1)}, f32[128]{0:T(128)}, u32[]{:S(2)}) copy-start(f32[128]{0:T(128)} %dynamic_slice.15) | copy-start | bytes 1540
  1196.7 100.1 %copy-start.52 = (bf16[3,128]{1,0:T(4,128)(2,1)S(1)}, bf16[3,128]{1,0:T(4,128)(2,1)}, u32[]{:S(2)}) copy-start(bf16[3,128]{1,0:T(4,128)(2,1)} %pad_maximum_fusion.3) | copy-start | bytes 2308
  1196.7 100.1 %copy-start.59 = (bf16[128]{0:T(256)(128)(2,1)S(1)}, bf16[128]{0:T(256)(128)(2,1)}, u32[]{:S(2)}) copy-start(bf16[128]{0:T(256)(128)(2,1)} %get-tuple-element.50) | copy-start | bytes 772
  (56 other events, 977.2 us)
Sparse Core Ops, SparseCore 0:
  9.9 57.6 all-gather.7
  90.6 539.6 all-gather.13
  632.1 51.2 all-gather.9
  749.9 102.1 reduce-scatter.2
  884.4 56.0 all-gather.11
  1021.9 166.8 all-reduce.9
  1192.3 101.1 reduce-scatter.4
  1295.4 516.2 all-gather.15
